TPU v7x, 32 devices: a whole 2x2x4 slice. The times are simulated.
32 devices in a mesh: patch: 16 (over z, x, core), sec: 2 (over y).
Axes of the slice: x: 2, y: 2, z: 4, core: 2. Of those that a mesh axis runs over, the one named last changes fastest.
Arguments:
- concentration: float32 [16, 8, 128, 128], P('patch', 'sec'), may hold values from -1 to 1
- partner: int32 [16, 4], replicated, may hold values from 0 to 15, as said below
- face_id: int32 [16, 4], replicated, may hold values from 0 to 3, as said below
- flip: int32 [16, 4], replicated, may hold values from 0 to 1, as said below
Outputs:
- evolved: float32 [16, 8, 128, 128], P('patch', 'sec')
Inputs may be any that keep to these rules, and one draw needn't show every extreme that they name: Across face f of patch p lies face face_id[p, f] of patch partner[p, f], and across that face lies face f of patch p again; the four partners of a patch are four different patches, none of them p itself. `face_id`: see partner. `flip`: equal on the two sides of an interface.
All inputs are finite; a program needn't handle non-finite values.
Results may differ from a plain program's by a relative error of at most 0.0001.
Values sent between devices are 32-bit elements; how exact they have to be, the bound alone decides.
No kernel may reach another device: no remote copies, remote signals or barrier semaphores. Data moves between devices by JAX's collectives and lax.ppermute only.
A program may use at most 64 MiB of HBM per device.

v0:
```python
import jax
import jax.numpy as jnp
from jax import lax
from jax.sharding import PartitionSpec as P

ITERS = 3
STEPS = 2
MASS_BAND = (2416.0 / 5040.0, 1191.0 / 5040.0, 120.0 / 5040.0, 1.0 / 5040.0)
STIFF_BAND = (2.0 / 3.0, -0.125, -0.2, -1.0 / 120.0)
PENALTY = 2.0
TIME_STEP = 1.0
STABILIZER = 2.0
GRADIENT_ENERGY = 0.5


def padded_2(cells, sides, width):
    for axis, dim in sides:
        count = lax.axis_size(axis)
        ends = count - 1
        head = lax.slice_in_dim(cells, 0, width, axis=dim)
        tail = lax.slice_in_dim(cells, cells.shape[dim] - width, cells.shape[dim], axis=dim)
        cells = jnp.concatenate(
            [
                lax.ppermute(tail, axis, [(i, (i + 1) % count) for i in range(ends)]),
                cells,
                lax.ppermute(head, axis, [((i + 1) % count, i) for i in range(ends)]),
            ],
            axis=dim,
        )
    return cells


def banded_padded(padded, coefficients, along, length):
    summed = coefficients[0] * lax.slice_in_dim(padded, 3, 3 + length, axis=along)
    for offset in range(1, 4):
        lower = lax.slice_in_dim(padded, 3 - offset, 3 - offset + length, axis=along)
        upper = lax.slice_in_dim(padded, 3 + offset, 3 + offset + length, axis=along)
        summed = summed + coefficients[offset] * (lower + upper)
    return summed


def banded(field, coefficients, along):
    length = field.shape[along]
    widths = [(0, 0)] * field.ndim
    widths[along] = (3, 3)
    return banded_padded(jnp.pad(field, widths), coefficients, along, length)


def tensor_parts(mass_third, stiff_third, first_axis, second_axis):
    mass_both = banded(mass_third, MASS_BAND, second_axis)
    stiff_second = banded(mass_third, STIFF_BAND, second_axis)
    mixed_second = banded(stiff_third, MASS_BAND, second_axis)
    stiffness = banded(mass_both, STIFF_BAND, first_axis) + banded(
        stiff_second + mixed_second, MASS_BAND, first_axis
    )
    return (mass_both, stiffness)


def face_traces(field):
    return jnp.stack(
        [field[..., 0, :], field[..., -1, :], field[..., :, 0], field[..., :, -1]],
        axis=field.ndim - 3,
    )


def add_penalty(stiffness, mismatch, face_axis):
    pieces = [lax.index_in_dim(mismatch, number, face_axis, keepdims=False) for number in range(4)]
    stiffness = stiffness.at[..., 0, :].add(PENALTY * pieces[0])
    stiffness = stiffness.at[..., -1, :].add(PENALTY * pieces[1])
    stiffness = stiffness.at[..., :, 0].add(PENALTY * pieces[2])
    stiffness = stiffness.at[..., :, -1].add(PENALTY * pieces[3])
    return stiffness


def partner_traces(traces, partner_row, face_row, flip_row):
    all_traces = lax.all_gather(traces[None], "patch", axis=0, tiled=True)
    picked = all_traces[partner_row, face_row]
    return jnp.where(flip_row[:, None, None] == 1, picked[..., ::-1], picked)


def stiffness_local(field, tables, with_mass):
    length = field.shape[0]
    padded = padded_2(field, (("sec", 0),), 3)
    mass_third = banded_padded(padded, MASS_BAND, 0, length)
    stiff_third = banded_padded(padded, STIFF_BAND, 0, length)
    mass_both, stiffness = tensor_parts(mass_third, stiff_third, 1, 2)
    traces = face_traces(field)
    others = partner_traces(traces, tables[0], tables[1], tables[2])
    stiffness = add_penalty(stiffness, traces - others, 0)
    mass_full = banded(mass_both, MASS_BAND, 1) if with_mass else None
    return (mass_full, stiffness)


def operate(direction, tables):
    mass_full, stiff_one = stiffness_local(direction, tables, True)
    unused, stiff_two = stiffness_local(stiff_one, tables, False)
    return mass_full + TIME_STEP * STABILIZER * stiff_one + TIME_STEP * GRADIENT_ENERGY * stiff_two


def squares(residual):
    return lax.psum(jnp.sum(residual * residual), ("patch", "sec"))


def shards(concentration, partner, face_id, flip):
    patch_now = lax.axis_index("patch")
    tables = (
        lax.dynamic_index_in_dim(partner, patch_now, 0, keepdims=False),
        lax.dynamic_index_in_dim(face_id, patch_now, 0, keepdims=False),
        lax.dynamic_index_in_dim(flip, patch_now, 0, keepdims=False),
    )
    iterate = concentration[0]
    for section in range(STEPS):
        current = iterate
        unused, curvature = stiffness_local(current, tables, False)
        potential = current * current * current - current + GRADIENT_ENERGY * curvature
        unused, flux = stiffness_local(potential, tables, False)
        residual = -TIME_STEP * flux
        direction = residual
        norm_now = squares(residual)
        for iteration in range(ITERS):
            image = operate(direction, tables)
            step_size = norm_now / lax.psum(jnp.sum(direction * image), ("patch", "sec"))
            iterate = iterate + step_size * direction
            if iteration + 1 < ITERS:
                residual = residual - step_size * image
                norm_next = squares(residual)
                direction = residual + norm_next / norm_now * direction
                norm_now = norm_next
    return iterate[None]


def solution(mesh):
    placed = (P("patch", "sec", None, None), P(), P(), P())
    return jax.shard_map(
        shards, mesh=mesh, in_specs=placed, out_specs=P("patch", "sec", None, None), check_vma=False
    )
```

profile of v0, /device:TPU:14, one launch (start us, length us, event | category | flops | bytes accessed | tf_op | source)
XLA Modules:
  0.0 1101.7 jit_solution(2193271219574866490)
XLA Ops:
  46.9 21.8 %all-gather.1 = f32[64,4,128]{2,1,0:T(4,128)S(1)} all-gather(f32[4,4,128]{2,1,0:T(4,128)S(1)} %pad_maximum_fusion.33), channel_id=3, replica_groups=mesh['patch'=16,'sec'=2] {'patch'}, dimensions={0}, use_global_device_ids=true | all-gather | bytes 139264 | tf_op jit(solution)/shard_map/all_gather | solution.py:76
  80.6 17.5 %all-gather.2 = f32[64,4,128]{2,1,0:T(4,128)S(1)} all-gather(f32[4,4,128]{2,1,0:T(4,128)S(1)} %pad_maximum_fusion.34), channel_id=4, replica_groups=mesh['patch'=16,'sec'=2] {'patch'}, dimensions={0}, use_global_device_ids=true | all-gather | bytes 139264 | tf_op jit(solution)/shard_map/all_gather | solution.py:76
  122.4 19.8 %all-gather.3 = f32[64,4,128]{2,1,0:T(4,128)S(1)} all-gather(f32[4,4,128]{2,1,0:T(4,128)S(1)} %pad_maximum_fusion.35), channel_id=5, replica_groups=mesh['patch'=16,'sec'=2] {'patch'}, dimensions={0}, use_global_device_ids=true | all-gather | bytes 139264 | tf_op jit(solution)/shard_map/all_gather | solution.py:76
  161.5 44.3 %all-reduce.65 = (f32[]{:T(128)}, f32[]{:T(128)}) all-reduce(f32[]{:T(128)} %get-tuple-element.776, f32[]{:T(128)} %get-tuple-element.775), channel_id=1, replica_groups=mesh['patch'=16,'sec'=2] {'patch','sec'}, use_global_device_ids=true, to_apply=%region_1.2 | all-reduce | flops 2 | bytes 16 | tf_op jit(solution)/shard_map/psum | solution.py:101
  207.8 38.7 %psum.86 = f32[]{:T(128)} all-reduce(f32[]{:T(128)} %get-tuple-element.825), channel_id=1, replica_groups=mesh['patch'=16,'sec'=2] {'patch','sec'}, use_global_device_ids=true, to_apply=%region_5.6 | all-reduce | flops 1 | bytes 8 | tf_op jit(solution)/shard_map/psum | solution.py:101
  253.1 16.2 %all-gather.4 = f32[64,4,128]{2,1,0:T(4,128)S(1)} all-gather(f32[4,4,128]{2,1,0:T(4,128)S(1)} %pad_maximum_fusion.36), channel_id=6, replica_groups=mesh['patch'=16,'sec'=2] {'patch'}, dimensions={0}, use_global_device_ids=true | all-gather | bytes 139264 | tf_op jit(solution)/shard_map/all_gather | solution.py:76
  294.1 20.9 %all-gather.5 = f32[64,4,128]{2,1,0:T(4,128)S(1)} all-gather(f32[4,4,128]{2,1,0:T(4,128)S(1)} %pad_maximum_fusion.37), channel_id=7, replica_groups=mesh['patch'=16,'sec'=2] {'patch'}, dimensions={0}, use_global_device_ids=true | all-gather | bytes 139264 | tf_op jit(solution)/shard_map/all_gather | solution.py:76
  334.1 44.3 %psum.87 = f32[]{:T(128)} all-reduce(f32[]{:T(128)} %get-tuple-element.817), channel_id=1, replica_groups=mesh['patch'=16,'sec'=2] {'patch','sec'}, use_global_device_ids=true, to_apply=%region_7.8 | all-reduce | flops 1 | bytes 8 | tf_op jit(solution)/shard_map/psum | solution.py:122
  380.4 38.6 %psum.88 = f32[]{:T(128)} all-reduce(f32[]{:T(128)} %multiply_reduce_fusion.7), channel_id=1, replica_groups=mesh['patch'=16,'sec'=2] {'patch','sec'}, use_global_device_ids=true, to_apply=%region_9.10 | all-reduce | flops 1 | bytes 8 | tf_op jit(solution)/shard_map/psum | solution.py:101
  425.6 16.3 %all-gather.6 = f32[64,4,128]{2,1,0:T(4,128)S(1)} all-gather(f32[4,4,128]{2,1,0:T(4,128)S(1)} %pad_maximum_fusion.38), channel_id=8, replica_groups=mesh['patch'=16,'sec'=2] {'patch'}, dimensions={0}, use_global_device_ids=true | all-gather | bytes 139264 | tf_op jit(solution)/shard_map/all_gather | solution.py:76
  466.7 21.2 %all-gather.7 = f32[64,4,128]{2,1,0:T(4,128)S(1)} all-gather(f32[4,4,128]{2,1,0:T(4,128)S(1)} %pad_maximum_fusion.39), channel_id=9, replica_groups=mesh['patch'=16,'sec'=2] {'patch'}, dimensions={0}, use_global_device_ids=true | all-gather | bytes 139264 | tf_op jit(solution)/shard_map/all_gather | solution.py:76
  507.0 44.3 %psum.89 = f32[]{:T(128)} all-reduce(f32[]{:T(128)} %multiply_reduce_fusion.6), channel_id=1, replica_groups=mesh['patch'=16,'sec'=2] {'patch','sec'}, use_global_device_ids=true, to_apply=%region_11.12 | all-reduce | flops 1 | bytes 8 | tf_op jit(solution)/shard_map/psum | solution.py:122
  594.6 21.2 %all-gather.9 = f32[64,4,128]{2,1,0:T(4,128)S(1)} all-gather(f32[4,4,128]{2,1,0:T(4,128)S(1)} %pad_maximum_fusion.41), channel_id=11, replica_groups=mesh['patch'=16,'sec'=2] {'patch'}, dimensions={0}, use_global_device_ids=true | all-gather | bytes 139264 | tf_op jit(solution)/shard_map/all_gather | solution.py:76
  640.3 17.7 %all-gather.10 = f32[64,4,128]{2,1,0:T(4,128)S(1)} all-gather(f32[4,4,128]{2,1,0:T(4,128)S(1)} %pad_maximum_fusion.42), channel_id=12, replica_groups=mesh['patch'=16,'sec'=2] {'patch'}, dimensions={0}, use_global_device_ids=true | all-gather | bytes 139264 | tf_op jit(solution)/shard_map/all_gather | solution.py:76
  683.9 19.9 %all-gather.11 = f32[64,4,128]{2,1,0:T(4,128)S(1)} all-gather(f32[4,4,128]{2,1,0:T(4,128)S(1)} %pad_maximum_fusion.43), channel_id=13, replica_groups=mesh['patch'=16,'sec'=2] {'patch'}, dimensions={0}, use_global_device_ids=true | all-gather | bytes 139264 | tf_op jit(solution)/shard_map/all_gather | solution.py:76
  722.7 44.4 %all-reduce.64 = (f32[]{:T(128)}, f32[]{:T(128)}) all-reduce(f32[]{:T(128)} %get-tuple-element.774, f32[]{:T(128)} %get-tuple-element.773), channel_id=1, replica_groups=mesh['patch'=16,'sec'=2] {'patch','sec'}, use_global_device_ids=true, to_apply=%region_13.14 | all-reduce | flops 2 | bytes 16 | tf_op jit(solution)/shard_map/psum | solution.py:101
  769.4 38.6 %psum.92 = f32[]{:T(128)} all-reduce(f32[]{:T(128)} %get-tuple-element.797), channel_id=1, replica_groups=mesh['patch'=16,'sec'=2] {'patch','sec'}, use_global_device_ids=true, to_apply=%region_17.18 | all-reduce | flops 1 | bytes 8 | tf_op jit(solution)/shard_map/psum | solution.py:101
  814.3 16.2 %all-gather.12 = f32[64,4,128]{2,1,0:T(4,128)S(1)} all-gather(f32[4,4,128]{2,1,0:T(4,128)S(1)} %pad_maximum_fusion.44), channel_id=14, replica_groups=mesh['patch'=16,'sec'=2] {'patch'}, dimensions={0}, use_global_device_ids=true | all-gather | bytes 139264 | tf_op jit(solution)/shard_map/all_gather | solution.py:76
  855.1 20.9 %all-gather.13 = f32[64,4,128]{2,1,0:T(4,128)S(1)} all-gather(f32[4,4,128]{2,1,0:T(4,128)S(1)} %pad_maximum_fusion.45), channel_id=15, replica_groups=mesh['patch'=16,'sec'=2] {'patch'}, dimensions={0}, use_global_device_ids=true | all-gather | bytes 139264 | tf_op jit(solution)/shard_map/all_gather | solution.py:76
  895.7 44.2 %psum.93 = f32[]{:T(128)} all-reduce(f32[]{:T(128)} %multiply_reduce_fusion.2), channel_id=1, replica_groups=mesh['patch'=16,'sec'=2] {'patch','sec'}, use_global_device_ids=true, to_apply=%region_19.20 | all-reduce | flops 1 | bytes 8 | tf_op jit(solution)/shard_map/psum | solution.py:122
  942.0 38.6 %psum.94 = f32[]{:T(128)} all-reduce(f32[]{:T(128)} %get-tuple-element.789), channel_id=1, replica_groups=mesh['patch'=16,'sec'=2] {'patch','sec'}, use_global_device_ids=true, to_apply=%region_21.22 | all-reduce | flops 1 | bytes 8 | tf_op jit(solution)/shard_map/psum | solution.py:101
  987.0 16.3 %all-gather.14 = f32[64,4,128]{2,1,0:T(4,128)S(1)} all-gather(f32[4,4,128]{2,1,0:T(4,128)S(1)} %pad_maximum_fusion.46), channel_id=16, replica_groups=mesh['patch'=16,'sec'=2] {'patch'}, dimensions={0}, use_global_device_ids=true | all-gather | bytes 139264 | tf_op jit(solution)/shard_map/all_gather | solution.py:76
  1027.8 20.7 %all-gather.15 = f32[64,4,128]{2,1,0:T(4,128)S(1)} all-gather(f32[4,4,128]{2,1,0:T(4,128)S(1)} %pad_maximum_fusion.47), channel_id=17, replica_groups=mesh['patch'=16,'sec'=2] {'patch'}, dimensions={0}, use_global_device_ids=true | all-gather | bytes 139264 | tf_op jit(solution)/shard_map/all_gather | solution.py:76
  1054.7 44.3 %psum.95 = f32[]{:T(128)} all-reduce(f32[]{:T(128)} %multiply_reduce_fusion), channel_id=1, replica_groups=mesh['patch'=16,'sec'=2] {'patch','sec'}, use_global_device_ids=true, to_apply=%region_23.24 | all-reduce | flops 1 | bytes 8 | tf_op jit(solution)/shard_map/psum | solution.py:122
  (465 shorter events, 398.9 us)
Async XLA Ops:
  1.2 22.4 %collective-permute-start.1 = (f32[3,128,128]{1,0,2:T(4,128)S(1)}, f32[3,128,128]{1,0,2:T(4,128)S(1)}, u32[]{:S(2)}, u32[]{:S(2)}) collective-permute-start(f32[3,128,128]{1,0,2:T(4,128)S(1)} %get-tuple-element.957), channel_id=1, source_target_pairs={{1,0},{3,2},{5,4},{7,6},{9,8},{11,10},{13,12},{15,14},{17,16},{19,... | collective-permute-start | bytes 589832 | tf_op jit(solution)/shard_map/ppermute | solution.py:26
  41.1 28.7 %collective-permute-start.3 = (f32[3,128,128]{2,0,1:T(4,128)S(1)}, f32[3,128,128]{2,0,1:T(4,128)S(1)}, u32[]{:S(2)}, u32[]{:S(2)}) collective-permute-start(f32[3,128,128]{2,0,1:T(4,128)S(1)} %get-tuple-element.949), channel_id=1, source_target_pairs={{1,0},{3,2},{5,4},{7,6},{9,8},{11,10},{13,12},{15,14},{17,16},{19,... | collective-permute-start | bytes 589832 | tf_op jit(solution)/shard_map/ppermute | solution.py:26
  45.6 24.1 %collective-permute-start.2 = (f32[3,128,128]{2,0,1:T(4,128)S(1)}, f32[3,128,128]{2,0,1:T(4,128)S(1)}, u32[]{:S(2)}, u32[]{:S(2)}) collective-permute-start(f32[3,128,128]{2,0,1:T(4,128)S(1)} %get-tuple-element.948), channel_id=1, source_target_pairs={{0,1},{2,3},{4,5},{6,7},{8,9},{10,11},{12,13},{14,15},{16,17},{18,... | collective-permute-start | bytes 589832 | tf_op jit(solution)/shard_map/ppermute | solution.py:24
  74.5 24.4 %collective-permute-start.5 = (f32[3,128,128]{1,0,2:T(4,128)S(1)}, f32[3,128,128]{1,0,2:T(4,128)S(1)}, u32[]{:S(2)}, u32[]{:S(2)}) collective-permute-start(f32[3,128,128]{1,0,2:T(4,128)S(1)} %get-tuple-element.945), channel_id=1, source_target_pairs={{1,0},{3,2},{5,4},{7,6},{9,8},{11,10},{13,12},{15,14},{17,16},{19,... | collective-permute-start | bytes 589832 | tf_op jit(solution)/shard_map/ppermute | solution.py:26
  116.3 27.1 %collective-permute-start.7 = (f32[3,128,128]{1,0,2:T(4,128)S(1)}, f32[3,128,128]{1,0,2:T(4,128)S(1)}, u32[]{:S(2)}, u32[]{:S(2)}) collective-permute-start(f32[3,128,128]{1,0,2:T(4,128)S(1)} %get-tuple-element.937), channel_id=1, source_target_pairs={{1,0},{3,2},{5,4},{7,6},{9,8},{11,10},{13,12},{15,14},{17,16},{19,... | collective-permute-start | bytes 589832 | tf_op jit(solution)/shard_map/ppermute | solution.py:26
  120.9 22.5 %collective-permute-start.6 = (f32[3,128,128]{1,0,2:T(4,128)S(1)}, f32[3,128,128]{1,0,2:T(4,128)S(1)}, u32[]{:S(2)}, u32[]{:S(2)}) collective-permute-start(f32[3,128,128]{1,0,2:T(4,128)S(1)} %get-tuple-element.936), channel_id=1, source_target_pairs={{0,1},{2,3},{4,5},{6,7},{8,9},{10,11},{12,13},{14,15},{16,17},{18,... | collective-permute-start | bytes 589832 | tf_op jit(solution)/shard_map/ppermute | solution.py:24
  248.2 22.2 %collective-permute-start.9 = (f32[3,128,128]{1,0,2:T(4,128)S(1)}, f32[3,128,128]{1,0,2:T(4,128)S(1)}, u32[]{:S(2)}, u32[]{:S(2)}) collective-permute-start(f32[3,128,128]{1,0,2:T(4,128)S(1)} %get-tuple-element.931), channel_id=1, source_target_pairs={{1,0},{3,2},{5,4},{7,6},{9,8},{11,10},{13,12},{15,14},{17,16},{19,... | collective-permute-start | bytes 589832 | tf_op jit(solution)/shard_map/ppermute | solution.py:26
  287.9 28.2 %collective-permute-start.11 = (f32[3,128,128]{1,0,2:T(4,128)}, f32[3,128,128]{1,0,2:T(4,128)S(1)}, u32[]{:S(2)}, u32[]{:S(2)}) collective-permute-start(f32[3,128,128]{1,0,2:T(4,128)} %get-tuple-element.923), channel_id=1, source_target_pairs={{1,0},{3,2},{5,4},{7,6},{9,8},{11,10},{13,12},{15,14},{17,16},{19,... | collective-permute-start | bytes 589832 | tf_op jit(solution)/shard_map/ppermute | solution.py:26
  292.5 23.6 %collective-permute-start.10 = (f32[3,128,128]{1,0,2:T(4,128)S(1)}, f32[3,128,128]{1,0,2:T(4,128)S(1)}, u32[]{:S(2)}, u32[]{:S(2)}) collective-permute-start(f32[3,128,128]{1,0,2:T(4,128)S(1)} %get-tuple-element.922), channel_id=1, source_target_pairs={{0,1},{2,3},{4,5},{6,7},{8,9},{10,11},{12,13},{14,15},{16,17},{18,... | collective-permute-start | bytes 589832 | tf_op jit(solution)/shard_map/ppermute | solution.py:24
  420.7 22.4 %collective-permute-start.13 = (f32[3,128,128]{1,0,2:T(4,128)S(1)}, f32[3,128,128]{1,0,2:T(4,128)S(1)}, u32[]{:S(2)}, u32[]{:S(2)}) collective-permute-start(f32[3,128,128]{1,0,2:T(4,128)S(1)} %get-tuple-element.917), channel_id=1, source_target_pairs={{1,0},{3,2},{5,4},{7,6},{9,8},{11,10},{13,12},{15,14},{17,16},{19,... | collective-permute-start | bytes 589832 | tf_op jit(solution)/shard_map/ppermute | solution.py:26
  460.6 28.4 %collective-permute-start.15 = (f32[3,128,128]{1,0,2:T(4,128)}, f32[3,128,128]{1,0,2:T(4,128)S(1)}, u32[]{:S(2)}, u32[]{:S(2)}) collective-permute-start(f32[3,128,128]{1,0,2:T(4,128)} %get-tuple-element.909), channel_id=1, source_target_pairs={{1,0},{3,2},{5,4},{7,6},{9,8},{11,10},{13,12},{15,14},{17,16},{19,... | collective-permute-start | bytes 589832 | tf_op jit(solution)/shard_map/ppermute | solution.py:26
  465.2 23.8 %collective-permute-start.14 = (f32[3,128,128]{1,0,2:T(4,128)S(1)}, f32[3,128,128]{1,0,2:T(4,128)S(1)}, u32[]{:S(2)}, u32[]{:S(2)}) collective-permute-start(f32[3,128,128]{1,0,2:T(4,128)S(1)} %get-tuple-element.908), channel_id=1, source_target_pairs={{0,1},{2,3},{4,5},{6,7},{8,9},{10,11},{12,13},{14,15},{16,17},{18,... | collective-permute-start | bytes 589832 | tf_op jit(solution)/shard_map/ppermute | solution.py:24
  588.5 28.5 %collective-permute-start.19 = (f32[3,128,128]{1,0,2:T(4,128)S(1)}, f32[3,128,128]{1,0,2:T(4,128)S(1)}, u32[]{:S(2)}, u32[]{:S(2)}) collective-permute-start(f32[3,128,128]{1,0,2:T(4,128)S(1)} %get-tuple-element.895), channel_id=1, source_target_pairs={{1,0},{3,2},{5,4},{7,6},{9,8},{11,10},{13,12},{15,14},{17,16},{19,... | collective-permute-start | bytes 589832 | tf_op jit(solution)/shard_map/ppermute | solution.py:26
  593.1 23.9 %collective-permute-start.18 = (f32[3,128,128]{1,0,2:T(4,128)S(1)}, f32[3,128,128]{1,0,2:T(4,128)S(1)}, u32[]{:S(2)}, u32[]{:S(2)}) collective-permute-start(f32[3,128,128]{1,0,2:T(4,128)S(1)} %get-tuple-element.894), channel_id=1, source_target_pairs={{0,1},{2,3},{4,5},{6,7},{8,9},{10,11},{12,13},{14,15},{16,17},{18,... | collective-permute-start | bytes 589832 | tf_op jit(solution)/shard_map/ppermute | solution.py:24
  634.2 25.0 %collective-permute-start.21 = (f32[3,128,128]{1,0,2:T(4,128)S(1)}, f32[3,128,128]{1,0,2:T(4,128)S(1)}, u32[]{:S(2)}, u32[]{:S(2)}) collective-permute-start(f32[3,128,128]{1,0,2:T(4,128)S(1)} %get-tuple-element.887), channel_id=1, source_target_pairs={{1,0},{3,2},{5,4},{7,6},{9,8},{11,10},{13,12},{15,14},{17,16},{19,... | collective-permute-start | bytes 589832 | tf_op jit(solution)/shard_map/ppermute | solution.py:26
  638.8 20.4 %collective-permute-start.20 = (f32[3,128,128]{1,0,2:T(4,128)S(1)}, f32[3,128,128]{1,0,2:T(4,128)S(1)}, u32[]{:S(2)}, u32[]{:S(2)}) collective-permute-start(f32[3,128,128]{1,0,2:T(4,128)S(1)} %get-tuple-element.886), channel_id=1, source_target_pairs={{0,1},{2,3},{4,5},{6,7},{8,9},{10,11},{12,13},{14,15},{16,17},{18,... | collective-permute-start | bytes 589832 | tf_op jit(solution)/shard_map/ppermute | solution.py:24
  677.8 27.3 %collective-permute-start.23 = (f32[3,128,128]{1,0,2:T(4,128)}, f32[3,128,128]{1,0,2:T(4,128)S(1)}, u32[]{:S(2)}, u32[]{:S(2)}) collective-permute-start(f32[3,128,128]{1,0,2:T(4,128)} %get-tuple-element.879), channel_id=1, source_target_pairs={{1,0},{3,2},{5,4},{7,6},{9,8},{11,10},{13,12},{15,14},{17,16},{19,... | collective-permute-start | bytes 589832 | tf_op jit(solution)/shard_map/ppermute | solution.py:26
  682.3 22.7 %collective-permute-start.22 = (f32[3,128,128]{1,0,2:T(4,128)S(1)}, f32[3,128,128]{1,0,2:T(4,128)S(1)}, u32[]{:S(2)}, u32[]{:S(2)}) collective-permute-start(f32[3,128,128]{1,0,2:T(4,128)S(1)} %get-tuple-element.878), channel_id=1, source_target_pairs={{0,1},{2,3},{4,5},{6,7},{8,9},{10,11},{12,13},{14,15},{16,17},{18,... | collective-permute-start | bytes 589832 | tf_op jit(solution)/shard_map/ppermute | solution.py:24
  809.6 21.9 %collective-permute-start.25 = (f32[3,128,128]{2,0,1:T(4,128)S(1)}, f32[3,128,128]{2,0,1:T(4,128)S(1)}, u32[]{:S(2)}, u32[]{:S(2)}) collective-permute-start(f32[3,128,128]{2,0,1:T(4,128)S(1)} %get-tuple-element.871), channel_id=1, source_target_pairs={{1,0},{3,2},{5,4},{7,6},{9,8},{11,10},{13,12},{15,14},{17,16},{19,... | collective-permute-start | bytes 589832 | tf_op jit(solution)/shard_map/ppermute | solution.py:26
  849.1 28.0 %collective-permute-start.27 = (f32[3,128,128]{2,0,1:T(4,128)S(1)}, f32[3,128,128]{2,0,1:T(4,128)S(1)}, u32[]{:S(2)}, u32[]{:S(2)}) collective-permute-start(f32[3,128,128]{2,0,1:T(4,128)S(1)} %get-tuple-element.863), channel_id=1, source_target_pairs={{1,0},{3,2},{5,4},{7,6},{9,8},{11,10},{13,12},{15,14},{17,16},{19,... | collective-permute-start | bytes 589832 | tf_op jit(solution)/shard_map/ppermute | solution.py:26
  853.7 23.5 %collective-permute-start.26 = (f32[3,128,128]{2,0,1:T(4,128)S(1)}, f32[3,128,128]{2,0,1:T(4,128)S(1)}, u32[]{:S(2)}, u32[]{:S(2)}) collective-permute-start(f32[3,128,128]{2,0,1:T(4,128)S(1)} %get-tuple-element.862), channel_id=1, source_target_pairs={{0,1},{2,3},{4,5},{6,7},{8,9},{10,11},{12,13},{14,15},{16,17},{18,... | collective-permute-start | bytes 589832 | tf_op jit(solution)/shard_map/ppermute | solution.py:24
  982.3 21.9 %collective-permute-start.29 = (f32[3,128,128]{2,0,1:T(4,128)S(1)}, f32[3,128,128]{2,0,1:T(4,128)S(1)}, u32[]{:S(2)}, u32[]{:S(2)}) collective-permute-start(f32[3,128,128]{2,0,1:T(4,128)S(1)} %get-tuple-element.855), channel_id=1, source_target_pairs={{1,0},{3,2},{5,4},{7,6},{9,8},{11,10},{13,12},{15,14},{17,16},{19,... | collective-permute-start | bytes 589832 | tf_op jit(solution)/shard_map/ppermute | solution.py:26
  1021.8 27.5 %collective-permute-start.31 = (f32[3,128,128]{2,0,1:T(4,128)S(1)}, f32[3,128,128]{2,0,1:T(4,128)S(1)}, u32[]{:S(2)}, u32[]{:S(2)}) collective-permute-start(f32[3,128,128]{2,0,1:T(4,128)S(1)} %get-tuple-element.847), channel_id=1, source_target_pairs={{1,0},{3,2},{5,4},{7,6},{9,8},{11,10},{13,12},{15,14},{17,16},{19,... | collective-permute-start | bytes 589832 | tf_op jit(solution)/shard_map/ppermute | solution.py:26
  1026.4 22.9 %collective-permute-start.30 = (f32[3,128,128]{2,0,1:T(4,128)S(1)}, f32[3,128,128]{2,0,1:T(4,128)S(1)}, u32[]{:S(2)}, u32[]{:S(2)}) collective-permute-start(f32[3,128,128]{2,0,1:T(4,128)S(1)} %get-tuple-element.846), channel_id=1, source_target_pairs={{0,1},{2,3},{4,5},{6,7},{8,9},{10,11},{12,13},{14,15},{16,17},{18,... | collective-permute-start | bytes 589832 | tf_op jit(solution)/shard_map/ppermute | solution.py:24
  (12 other events, 155.6 us)
where the time goes:
time: 1110 us; the launch traced here: 1100 us
  blocking collectives  716 us (65%)
  local copies, waits for them, and re-layouts  212 us (19%)
  starting transfers between devices  84.4 us (8%)
  other arithmetic  72.7 us (7%)
  between operations  15.9 us (1%)
    all_gather x16, blocking collectives, partner_traces(): all_traces = lax.all_gather(traces[None], 'patch', axis=0, tiled=True)  296 us
    psum x6, blocking collectives, squares(): return lax.psum(jnp.sum(residual * residual), ('patch', 'sec'))  243 us
    psum x4, blocking collectives, shards(): lax.psum(jnp.sum(direction * image), ('patch', 'sec'))  177 us
    scatter-add x13, local copies, waits for them, and re-layouts, add_penalty(): stiffness = stiffness.at[..., -1, :].add(PENALTY * pieces[1])  119 us
    ppermute x16, starting transfers between devices, padded_2(): lax.ppermute(head, axis, [((i + 1) % count, i) for i in range(ends)])  63.7 us
    add x42, other arithmetic, banded_padded(): summed = summed + coefficients[offset] * (lower + upper)  34.7 us
    scatter-add x10, local copies, waits for them, and re-layouts, add_penalty(): stiffness = stiffness.at[..., :, -1].add(PENALTY * pieces[3])  32.8 us
    scatter-add x11, local copies, waits for them, and re-layouts, add_penalty(): stiffness = stiffness.at[..., 0, :].add(PENALTY * pieces[0])  23.7 us
  transfers between devices with their start and end apart: 32, of which 0 were waited for; matrix products, arithmetic and copies ran while one was open for 2% of the time, Pallas kernels for 0%

commit v1 on v0

--- a/solution.py
+++ b/solution.py
@@ -73,7 +73,14 @@
 
 
 def partner_traces(traces, partner_row, face_row, flip_row):
-    all_traces = lax.all_gather(traces[None], "patch", axis=0, tiled=True)
+    ring = [traces[None]]
+    for hop in range(15):
+        ring.append(lax.ppermute(ring[-1], "patch", [(dev, (dev + 1) % 16) for dev in range(16)]))
+    all_traces = jnp.roll(
+        jnp.concatenate(ring[::-1], axis=0),
+        (lax.axis_index("patch") + 1) * ring[0].shape[0],
+        axis=0,
+    )
     picked = all_traces[partner_row, face_row]
     return jnp.where(flip_row[:, None, None] == 1, picked[..., ::-1], picked)
 

time: 1110 us -> 2180 us (1.96)
  waiting for transfers between devices: 0.08 us -> 1020 us
  starting transfers between devices: 84.4 us -> 258 us
  blocking collectives: 716 us -> 556 us
  local copies, waits for them, and re-layouts: 212 us -> 244 us
    ppermute x0 -> x240, waiting for transfers between devices: none -> 974 us  [partner_traces(): lax.ppermute(ring[-1], 'patch', [(dev, (dev + 1) % 16) for dev in range(1...]
    all_gather x16 -> x0, blocking collectives: 296 us -> none  [partner_traces(): all_traces = lax.all_gather(traces[None], 'patch', axis=0, tiled=True)]
    ppermute x0 -> x240, starting transfers between devices: none -> 160 us  [partner_traces(): lax.ppermute(ring[-1], 'patch', [(dev, (dev + 1) % 16) for dev in range(1...]
    psum x4, blocking collectives: 177 us -> 263 us  [shards(): lax.psum(jnp.sum(direction * image), ('patch', 'sec'))]
    psum x6, blocking collectives: 243 us -> 293 us  [squares(): return lax.psum(jnp.sum(residual * residual), ('patch', 'sec'))]
    scatter-add x13 -> x16, local copies, waits for them, and re-layouts: 119 us -> 161 us  [add_penalty(): stiffness = stiffness.at[..., -1, :].add(PENALTY * pieces[1])]
    scatter-add x10 -> x7, local copies, waits for them, and re-layouts: 32.8 us -> 11 us  [add_penalty(): stiffness = stiffness.at[..., :, -1].add(PENALTY * pieces[3])]
  transfers between devices with their start and end apart: 32 -> 272, of which waited for: 0 -> 254; matrix products, arithmetic and copies ran while one was open for 2% -> 1% of each run, Pallas kernels for 0% -> 0%
where the time goes in v1:
time: 2180 us; the launch traced here: 2160 us
  waiting for transfers between devices  1020 us (47%)
  blocking collectives  556 us (26%)
  starting transfers between devices  258 us (12%)
  local copies, waits for them, and re-layouts  244 us (11%)
  other arithmetic  73.8 us (3%)
    ppermute x240, waiting for transfers between devices, partner_traces(): lax.ppermute(ring[-1], 'patch', [(dev, (dev + 1) % 16) for dev in range(1...  974 us
    psum x6, blocking collectives, squares(): return lax.psum(jnp.sum(residual * residual), ('patch', 'sec'))  293 us
    psum x4, blocking collectives, shards(): lax.psum(jnp.sum(direction * image), ('patch', 'sec'))  263 us
    scatter-add x16, local copies, waits for them, and re-layouts, add_penalty(): stiffness = stiffness.at[..., -1, :].add(PENALTY * pieces[1])  161 us
    ppermute x240, starting transfers between devices, partner_traces(): lax.ppermute(ring[-1], 'patch', [(dev, (dev + 1) % 16) for dev in range(1...  160 us
    ppermute x16, starting transfers between devices, padded_2(): lax.ppermute(head, axis, [((i + 1) % count, i) for i in range(ends)])  77.1 us
  transfers between devices with their start and end apart: 272, of which 254 were waited for; matrix products, arithmetic and copies ran while one was open for 1% of the time, Pallas kernels for 0%

profile of v1, /device:TPU:14, one launch (start us, length us, event | category | flops | bytes accessed | tf_op | source)
XLA Modules:
  0.0 2164.5 jit_solution(17049075802559992741)
XLA Ops:
  70.0 10.8 scatter-add.215
  178.3 10.8 scatter-add.221
  286.7 10.8 scatter-add.229
  394.4 10.8 scatter-add.235
  406.7 65.8 %all-reduce.65 = (f32[]{:T(128)}, f32[]{:T(128)}) all-reduce(f32[]{:T(128)} %get-tuple-element.777, f32[]{:T(128)} %get-tuple-element.776), channel_id=1, replica_groups=mesh['patch'=16,'sec'=2] {'patch','sec'}, use_global_device_ids=true, to_apply=%region_1.3 | all-reduce | flops 2 | bytes 16 | tf_op jit(solution)/shard_map/psum | solution.py:108
  474.6 40.3 %psum.86 = f32[]{:T(128)} all-reduce(f32[]{:T(128)} %get-tuple-element.832), channel_id=1, replica_groups=mesh['patch'=16,'sec'=2] {'patch','sec'}, use_global_device_ids=true, to_apply=%region_5.7 | all-reduce | flops 1 | bytes 8 | tf_op jit(solution)/shard_map/psum | solution.py:108
  590.3 10.8 scatter-add.241
  696.2 10.8 scatter-add.249
  708.5 65.7 %psum.87 = f32[]{:T(128)} all-reduce(f32[]{:T(128)} %get-tuple-element.824), channel_id=1, replica_groups=mesh['patch'=16,'sec'=2] {'patch','sec'}, use_global_device_ids=true, to_apply=%region_7.9 | all-reduce | flops 1 | bytes 8 | tf_op jit(solution)/shard_map/psum | solution.py:129
  776.4 40.4 %psum.88 = f32[]{:T(128)} all-reduce(f32[]{:T(128)} %multiply_reduce_fusion.7), channel_id=1, replica_groups=mesh['patch'=16,'sec'=2] {'patch','sec'}, use_global_device_ids=true, to_apply=%region_9.11 | all-reduce | flops 1 | bytes 8 | tf_op jit(solution)/shard_map/psum | solution.py:108
  892.3 10.8 scatter-add.255
  998.1 10.8 scatter-add.261
  1010.4 65.7 %psum.89 = f32[]{:T(128)} all-reduce(f32[]{:T(128)} %multiply_reduce_fusion.6), channel_id=1, replica_groups=mesh['patch'=16,'sec'=2] {'patch','sec'}, use_global_device_ids=true, to_apply=%region_11.13 | all-reduce | flops 1 | bytes 8 | tf_op jit(solution)/shard_map/psum | solution.py:129
  1150.6 10.8 scatter-add.269
  1257.1 10.8 scatter-add.275
  1364.9 10.8 scatter-add.281
  1472.6 10.8 scatter-add.289
  1485.0 65.8 %all-reduce.64 = (f32[]{:T(128)}, f32[]{:T(128)}) all-reduce(f32[]{:T(128)} %get-tuple-element.775, f32[]{:T(128)} %get-tuple-element.774), channel_id=1, replica_groups=mesh['patch'=16,'sec'=2] {'patch','sec'}, use_global_device_ids=true, to_apply=%region_13.15 | all-reduce | flops 2 | bytes 16 | tf_op jit(solution)/shard_map/psum | solution.py:108
  1552.8 40.3 %psum.92 = f32[]{:T(128)} all-reduce(f32[]{:T(128)} %get-tuple-element.803), channel_id=1, replica_groups=mesh['patch'=16,'sec'=2] {'patch','sec'}, use_global_device_ids=true, to_apply=%region_17.19 | all-reduce | flops 1 | bytes 8 | tf_op jit(solution)/shard_map/psum | solution.py:108
  1668.6 10.8 scatter-add.295
  1774.4 10.8 scatter-add.301
  1786.7 65.7 %psum.93 = f32[]{:T(128)} all-reduce(f32[]{:T(128)} %get-tuple-element.795), channel_id=1, replica_groups=mesh['patch'=16,'sec'=2] {'patch','sec'}, use_global_device_ids=true, to_apply=%region_19.21 | all-reduce | flops 1 | bytes 8 | tf_op jit(solution)/shard_map/psum | solution.py:129
  1854.6 40.3 %psum.94 = f32[]{:T(128)} all-reduce(f32[]{:T(128)} %multiply_reduce_fusion.1), channel_id=1, replica_groups=mesh['patch'=16,'sec'=2] {'patch','sec'}, use_global_device_ids=true, to_apply=%region_21.23 | all-reduce | flops 1 | bytes 8 | tf_op jit(solution)/shard_map/psum | solution.py:108
  2096.1 65.7 %psum.95 = f32[]{:T(128)} all-reduce(f32[]{:T(128)} %multiply_reduce_fusion), channel_id=1, replica_groups=mesh['patch'=16,'sec'=2] {'patch','sec'}, use_global_device_ids=true, to_apply=%region_23.25 | all-reduce | flops 1 | bytes 8 | tf_op jit(solution)/shard_map/psum | solution.py:129
  (1224 shorter events, 1441.1 us)
Async XLA Ops:
  51.7 12.5 collective-permute-start
  53.0 11.2 collective-permute-start.1
  162.9 8.3 collective-permute-start.17
  164.2 8.4 collective-permute-start.18
  271.9 8.4 collective-permute-start.35
  380.2 8.4 collective-permute-start.52
  573.0 10.4 collective-permute-start.68
  574.3 10.3 collective-permute-start.69
  680.7 8.3 collective-permute-start.85
  682.0 8.4 collective-permute-start.86
  875.0 10.4 collective-permute-start.102
  876.3 10.3 collective-permute-start.103
  984.0 8.4 collective-permute-start.120
  1133.9 9.3 collective-permute-start.136
  1135.2 9.7 collective-permute-start.137
  1243.0 8.4 collective-permute-start.154
  1350.7 8.4 collective-permute-start.171
  1458.5 8.4 collective-permute-start.188
  1651.2 10.4 collective-permute-start.204
  1652.5 10.3 collective-permute-start.205
  1760.2 8.4 collective-permute-start.222
  1953.1 10.4 collective-permute-start.238
  1954.4 10.3 collective-permute-start.239
  2072.9 8.4 collective-permute-start.256
  (259 other events, 1313.1 us)
